TPU v7x, 32 devices: a whole 2x2x4 slice. The times are simulated.
32 devices in a mesh: dp: 2 (over x), row: 4 (over z), col: 4 (over y, core).
Axes of the slice: x: 2, y: 2, z: 4, core: 2. Of those that a mesh axis runs over, the one named last changes fastest.
Arguments:
- inputs: bfloat16 [1458, 1152], P('dp', 'row'), may hold values from -40 to 40
- pre_gain: float32 [1152], P('row'), may hold values from 0.5 to 1.5
- pre_shift: float32 [1152], P('row'), may hold values from -1.5 to 1.5
- joint_weight: bfloat16 [1152, 3456], P('row', 'col'), may hold values from -0.1875 to 0.1875
- joint_bias: float32 [4, 4, 144], P('col', 'row'), may hold values from -0.5 to 0.5
- merge_weight: bfloat16 [1152, 1152], P('col', 'row'), may hold values from -4 to 4
- merge_bias: float32 [1152], P('row'), may hold values from -2.5 to 2.5
- mid_gain: float32 [1152], P('row'), may hold values from 0.5 to 1.5
- mid_shift: float32 [1152], P('row'), may hold values from -1.5 to 1.5
- expand_weight: bfloat16 [1152, 4304], P('row', 'col'), may hold values from -0.1875 to 0.1875
- expand_bias: float32 [4304], P('col'), may hold values from -1.5 to 1.5
- reduce_weight: bfloat16 [4304, 1152], P('col', 'row'), may hold values from -0.09375 to 0.09375
- reduce_bias: float32 [1152], P('row'), may hold values from -2.5 to 2.5
- cotangent: bfloat16 [1458, 1152], P('dp', 'row'), may hold values from -6 to 6
Outputs:
- outputs: bfloat16 [1458, 1152], P('dp', 'row')
- inputs_grad: float32 [1458, 1152], P('dp', 'row')
- pre_gain_grad: float32 [1152], P('row')
- pre_shift_grad: float32 [1152], P('row')
- joint_weight_grad: float32 [1152, 3456], P('row', 'col')
- joint_bias_grad: float32 [4, 4, 144], P('col', 'row')
- merge_weight_grad: float32 [1152, 1152], P('col', 'row')
- merge_bias_grad: float32 [1152], P('row')
- mid_gain_grad: float32 [1152], P('row')
- mid_shift_grad: float32 [1152], P('row')
- expand_weight_grad: float32 [1152, 4304], P('row', 'col')
- expand_bias_grad: float32 [4304], P('col')
- reduce_weight_grad: float32 [4304, 1152], P('col', 'row')
- reduce_bias_grad: float32 [1152], P('row')
All inputs are finite; a program needn't handle non-finite values.
Results may differ from a plain program's by a relative error of at most 0.015.
Values may be sent and summed in bfloat16 or wider, within the bound.
No kernel may reach another device: no remote copies, remote signals or barrier semaphores. Data moves between devices by JAX's collectives and lax.ppermute only.
A program may use at most 64 MiB of HBM per device.

v0:
```python
import jax
import jax.numpy as jnp
from jax import lax
from jax.sharding import PartitionSpec as P

D = 1152
SEQ = 729
NORM_EPSILON = 1e-06
TANH_SLOPE = 0.7978845608028654
CUBIC_TERM = 0.044715


def gelu_value(preact):
    return (
        0.5
        * preact
        * (1.0 + jnp.tanh(TANH_SLOPE * (preact + CUBIC_TERM * preact * preact * preact)))
    )


def gelu_slope(preact):
    inner_tanh = jnp.tanh(TANH_SLOPE * (preact + CUBIC_TERM * preact * preact * preact))
    return 0.5 * (1.0 + inner_tanh) + 0.5 * preact * (
        1.0 - inner_tanh * inner_tanh
    ) * TANH_SLOPE * (1.0 + 3.0 * CUBIC_TERM * preact * preact)


def contract_rows(left, right):
    return lax.dot_general(
        left, right, (((0,), (0,)), ((), ())), preferred_element_type=jnp.float32
    )


def contract_cols(left, right):
    return lax.dot_general(
        left, right, (((1,), (1,)), ((), ())), preferred_element_type=jnp.float32
    )


def row_totals(first, second):
    return lax.psum((first, second), "row")


def col_total(partial_sum):
    return lax.psum(partial_sum, "col")


def ff_total(partial_sum):
    return lax.psum(partial_sum, "row")


def norm_forward(values, norm_gain, norm_shift):
    first, second = row_totals(
        jnp.sum(values, axis=-1, keepdims=True), jnp.sum(values * values, axis=-1, keepdims=True)
    )
    row_mean = first / D
    row_var = second / D - row_mean * row_mean
    inv_scale = lax.rsqrt(row_var + NORM_EPSILON)
    unit_rows = (values - row_mean) * inv_scale
    return (unit_rows, inv_scale, unit_rows * norm_gain + norm_shift)


def norm_backward(upstream, unit_rows, inv_scale, norm_gain):
    scaled = upstream * norm_gain
    first, second = row_totals(
        jnp.sum(scaled, axis=-1, keepdims=True), jnp.sum(scaled * unit_rows, axis=-1, keepdims=True)
    )
    return inv_scale * (scaled - first / D - unit_rows * (second / D))


def attend_image(query_rows, key_rows, value_rows):
    factor = query_rows.shape[-1] ** (-0.5)
    scores = (
        jnp.einsum("qhd,khd->hqk", query_rows, key_rows, preferred_element_type=jnp.float32)
        * factor
    )
    totals = jnp.log(jnp.sum(jnp.exp(scores), axis=-1))
    softmax_rows = jnp.exp(scores - totals[..., None]).astype(jnp.bfloat16)
    context = jnp.einsum(
        "hqk,khd->qhd", softmax_rows, value_rows, preferred_element_type=jnp.float32
    )
    return (context.astype(jnp.bfloat16), totals)


def attend_back(query_rows, key_rows, value_rows, context, totals, upstream):
    factor = query_rows.shape[-1] ** (-0.5)
    scores = (
        jnp.einsum("qhd,khd->hqk", query_rows, key_rows, preferred_element_type=jnp.float32)
        * factor
    )
    weights = jnp.exp(scores - totals[..., None])
    value_grad = jnp.einsum(
        "hqk,qhd->khd", weights.astype(jnp.bfloat16), upstream, preferred_element_type=jnp.float32
    )
    prob_grad = jnp.einsum("qhd,khd->hqk", upstream, value_rows, preferred_element_type=jnp.float32)
    row_delta = jnp.einsum("qhd,qhd->hq", upstream, context, preferred_element_type=jnp.float32)
    score_grad = (weights * (prob_grad - row_delta[..., None])).astype(jnp.bfloat16)
    query_grad = (
        jnp.einsum("hqk,khd->qhd", score_grad, key_rows, preferred_element_type=jnp.float32)
        * factor
    )
    key_grad = (
        jnp.einsum("hqk,qhd->khd", score_grad, query_rows, preferred_element_type=jnp.float32)
        * factor
    )
    return (query_grad, key_grad, value_grad)


def body(
    inputs,
    pre_gain,
    pre_shift,
    joint_weight,
    joint_bias,
    merge_weight,
    merge_bias,
    mid_gain,
    mid_shift,
    expand_weight,
    expand_bias,
    reduce_weight,
    reduce_bias,
    cotangent,
):
    token_count = inputs.shape[0]
    image_count = token_count // SEQ
    local_heads = joint_bias.shape[1]
    head_size = joint_bias.shape[2] // 2
    residual = inputs.astype(jnp.float32)
    unit_first, scale_first, normed_first = norm_forward(residual, pre_gain, pre_shift)
    normed_first = normed_first.astype(jnp.bfloat16)
    joint_part = jnp.dot(normed_first, joint_weight, preferred_element_type=jnp.float32)
    joint_sum = lax.psum_scatter(joint_part, "row", scatter_dimension=1, tiled=True)
    bias_pairs = joint_bias.reshape(local_heads, 2 * head_size)
    bias_rows = jnp.concatenate(
        [
            bias_pairs[:, :head_size],
            jnp.zeros((local_heads, head_size), jnp.float32),
            bias_pairs[:, head_size:],
        ],
        axis=1,
    ).reshape(-1)
    joint_rows = (joint_sum + bias_rows).astype(jnp.bfloat16)
    per_head = joint_rows.reshape(image_count, SEQ, local_heads, 3 * head_size)
    query_rows = per_head[..., :head_size]
    key_rows = per_head[..., head_size : 2 * head_size]
    value_rows = per_head[..., 2 * head_size :]
    context, totals = lax.map(
        lambda packed: attend_image(packed[0], packed[1], packed[2]),
        (query_rows, key_rows, value_rows),
    )
    context_flat = context.reshape(token_count, local_heads * head_size)
    context_group = lax.all_gather(context_flat, "row", axis=1, tiled=True)
    mixed_first = (
        residual
        + col_total(jnp.dot(context_group, merge_weight, preferred_element_type=jnp.float32))
        + merge_bias
    )
    unit_second, scale_second, normed_second = norm_forward(mixed_first, mid_gain, mid_shift)
    normed_second = normed_second.astype(jnp.bfloat16)
    hidden_pre = (
        ff_total(jnp.dot(normed_second, expand_weight, preferred_element_type=jnp.float32))
        + expand_bias
    )
    active = gelu_value(hidden_pre).astype(jnp.bfloat16)
    mixed_second = (
        mixed_first
        + col_total(jnp.dot(active, reduce_weight, preferred_element_type=jnp.float32))
        + reduce_bias
    )
    outputs = mixed_second.astype(jnp.bfloat16)
    grad_out = cotangent.astype(jnp.float32)
    reduce_weight_grad = contract_rows(active, cotangent)
    reduce_bias_grad = jnp.sum(grad_out, axis=0)
    hidden_grad = (
        ff_total(contract_cols(cotangent, reduce_weight)) * gelu_slope(hidden_pre)
    ).astype(jnp.bfloat16)
    expand_weight_grad = contract_rows(normed_second, hidden_grad)
    expand_bias_grad = jnp.sum(hidden_grad, axis=0, dtype=jnp.float32)
    normed_second_grad = col_total(contract_cols(hidden_grad, expand_weight))
    mid_gain_grad = jnp.sum(normed_second_grad * unit_second, axis=0)
    mid_shift_grad = jnp.sum(normed_second_grad, axis=0)
    mixed_grad = grad_out + norm_backward(normed_second_grad, unit_second, scale_second, mid_gain)
    mixed_low = mixed_grad.astype(jnp.bfloat16)
    merge_weight_grad = contract_rows(context_group, mixed_low)
    merge_bias_grad = jnp.sum(mixed_grad, axis=0)
    context_grad = lax.psum_scatter(
        contract_cols(mixed_low, merge_weight), "row", scatter_dimension=1, tiled=True
    ).astype(jnp.bfloat16)
    context_grad = context_grad.reshape(image_count, SEQ, local_heads, head_size)
    query_grad, key_grad, value_grad = lax.map(
        lambda packed: attend_back(
            packed[0], packed[1], packed[2], packed[3], packed[4], packed[5]
        ),
        (query_rows, key_rows, value_rows, context, totals, context_grad),
    )
    joint_grad = (
        jnp.concatenate([query_grad, key_grad, value_grad], axis=-1)
        .astype(jnp.bfloat16)
        .reshape(token_count, 3 * local_heads * head_size)
    )
    joint_bias_grad = jnp.concatenate(
        [jnp.sum(query_grad, axis=(0, 1)), jnp.sum(value_grad, axis=(0, 1))], axis=-1
    ).reshape(1, local_heads, 2 * head_size)
    joint_group = lax.all_gather(joint_grad, "row", axis=1, tiled=True)
    joint_weight_grad = contract_rows(normed_first, joint_group)
    normed_first_grad = col_total(contract_cols(joint_group, joint_weight))
    pre_gain_grad = jnp.sum(normed_first_grad * unit_first, axis=0)
    pre_shift_grad = jnp.sum(normed_first_grad, axis=0)
    inputs_grad = mixed_grad + norm_backward(normed_first_grad, unit_first, scale_first, pre_gain)
    (
        reduce_weight_grad,
        reduce_bias_grad,
        expand_weight_grad,
        expand_bias_grad,
        mid_gain_grad,
        mid_shift_grad,
        joint_weight_grad,
        joint_bias_grad,
        merge_weight_grad,
        merge_bias_grad,
        pre_gain_grad,
        pre_shift_grad,
    ) = lax.psum(
        (
            reduce_weight_grad,
            reduce_bias_grad,
            expand_weight_grad,
            expand_bias_grad,
            mid_gain_grad,
            mid_shift_grad,
            joint_weight_grad,
            joint_bias_grad,
            merge_weight_grad,
            merge_bias_grad,
            pre_gain_grad,
            pre_shift_grad,
        ),
        "dp",
    )
    return (
        outputs,
        inputs_grad,
        pre_gain_grad,
        pre_shift_grad,
        joint_weight_grad,
        joint_bias_grad,
        merge_weight_grad,
        merge_bias_grad,
        mid_gain_grad,
        mid_shift_grad,
        expand_weight_grad,
        expand_bias_grad,
        reduce_weight_grad,
        reduce_bias_grad,
    )


def solution(mesh):
    in_specs = (
        P("dp", "row"),
        P("row"),
        P("row"),
        P("row", "col"),
        P("col", "row", None),
        P("col", "row"),
        P("row"),
        P("row"),
        P("row"),
        P("row", "col"),
        P("col"),
        P("col", "row"),
        P("row"),
        P("dp", "row"),
    )
    out_specs = (
        P("dp", "row"),
        P("dp", "row"),
        P("row"),
        P("row"),
        P("row", "col"),
        P("col", "row", None),
        P("col", "row"),
        P("row"),
        P("row"),
        P("row"),
        P("row", "col"),
        P("col"),
        P("col", "row"),
        P("row"),
    )
    return jax.shard_map(body, mesh=mesh, in_specs=in_specs, out_specs=out_specs, check_vma=False)
```

profile of v0, /device:TPU:0, one launch (start us, length us, event | category | flops | bytes accessed | tf_op | source)
XLA Modules:
  0.0 673.6 jit_solution(1483904082346468682)
XLA Ops:
  7.2 0.0 reduce-scatter.3.cloned.1.call-start
  7.2 1.2 convert_reduce_fusion.1
  8.5 13.7 %all-reduce.4 = (f32[729,1]{0,1:T(1,128)S(1)}, f32[729,1]{0,1:T(1,128)S(1)}) all-reduce(f32[729,1]{0,1:T(1,128)S(1)} %broadcast_in_dim.57, f32[729,1]{0,1:T(1,128)S(1)} %broadcast_in_dim.58), channel_id=1, replica_groups=mesh['dp'=2,'row'=4,'col'=4] {'row'}, use_global_device_ids=true, to_apply=%region_1.0 | all-reduce | flops 1458 | bytes 11664 | tf_op jit(solution)/shard_map/psum | solution.py:41
  22.2 3.7 fusion.43
  26.0 0.0 reduce-scatter.3.cloned.1.call-update
  26.0 0.0 all-reduce.14.cloned.1.call-start
  26.0 0.1 pad.6.clone
  26.1 0.1 fusion.53
  26.2 0.1 pad_maximum_fusion.1
  26.3 50.8 %reduce-scatter.3.cloned.1.call-done = f32[729,216]{0,1:T(8,128)} async-done(((f32[729,864]{0,1:T(8,128)}), f32[729,216]{0,1:T(8,128)}) %reduce-scatter.3.cloned.1.call-update) | async-done | bytes 629872 | tf_op jit(solution)/shard_map/reduce_scatter | solution.py:133
  77.1 1.2 fusion.28
  78.3 0.6 exponential_reduce_fusion
  78.9 0.5 convolution_convert_fusion
  79.4 15.0 %all-gather = bf16[729,1,288]{0,2,1:T(8,128)(2,1)S(1)} all-gather(bf16[729,1,72]{0,2,1:T(8,128)(2,1)S(1)} %bitcast.72), channel_id=2, replica_groups=mesh['dp'=2,'row'=4,'col'=4] {'row'}, dimensions={2}, use_global_device_ids=true | all-gather | bytes 524880 | tf_op jit(solution)/shard_map/all_gather | solution.py:153
  94.4 0.8 copy-done.6
  95.2 1.3 fusion.26
  96.6 0.0 all-reduce.20.cloned.1.call-start
  96.7 4.1 fusion.59
  100.8 31.2 %all-reduce.14.cloned.1.call-done = f32[729,288]{0,1:T(8,128)} async-done(((f32[729,288]{0,1:T(8,128)}), f32[729,288]{0,1:T(8,128)}) %all-reduce.14.cloned.1.call-update) | async-done | bytes 839824 | tf_op jit(solution)/shard_map/psum | solution.py:45
  131.9 2.3 fusion.47
  134.2 11.8 %all-reduce.3 = (f32[729,1]{0,1:T(1,128)S(1)}, f32[729,1]{0,1:T(1,128)S(1)}) all-reduce(f32[729,1]{0,1:T(1,128)S(1)} %broadcast_in_dim.60, f32[729,1]{0,1:T(1,128)S(1)} %broadcast_in_dim.61), channel_id=1, replica_groups=mesh['dp'=2,'row'=4,'col'=4] {'row'}, use_global_device_ids=true, to_apply=%region_8.9 | all-reduce | flops 1458 | bytes 11664 | tf_op jit(solution)/shard_map/psum | solution.py:41
  146.1 4.1 fusion.46
  150.2 0.0 all-reduce.16.cloned.1.call-start
  150.3 231.6 %all-reduce.20.cloned.1.call-done = (f32[729,1076]{0,1:T(8,128)}, f32[729,1076]{0,1:T(8,128)}) async-done(((f32[729,1076]{0,1:T(8,128)}, f32[729,1076]{0,1:T(8,128)}), (f32[729,1076]{0,1:T(8,128)}, f32[729,1076]{0,1:T(8,128)})) %all-reduce.20.cloned.1.call-update) | async-done | bytes 6275248 | tf_op jit(solution)/shard_map/psum | solution.py:49
  381.9 5.9 convert_reduce_fusion
  387.8 1.2 copy-done.13
  389.0 1.7 fusion.60
  390.7 0.0 reduce-scatter.5.cloned.1.call-start
  390.8 34.7 %all-reduce.16.cloned.1.call-done = f32[729,288]{0,1:T(8,128)} async-done(((f32[729,288]{0,1:T(8,128)}), f32[729,288]{0,1:T(8,128)}) %all-reduce.16.cloned.1.call-update) | async-done | bytes 839824 | tf_op jit(solution)/shard_map/psum | solution.py:45
  425.4 1.8 multiply_reduce_fusion
  427.3 11.8 %all-reduce.2 = (f32[729,1]{0,1:T(1,128)S(1)}, f32[729,1]{0,1:T(1,128)S(1)}) all-reduce(f32[729,1]{0,1:T(1,128)S(1)} %broadcast_in_dim.63, f32[729,1]{0,1:T(1,128)S(1)} %broadcast_in_dim.62), channel_id=1, replica_groups=mesh['dp'=2,'row'=4,'col'=4] {'row'}, use_global_device_ids=true, to_apply=%region_18.19 | all-reduce | flops 1458 | bytes 11664 | tf_op jit(solution)/shard_map/psum | solution.py:41
  439.2 2.2 fusion.49
  441.3 1.0 copy-done.2
  442.3 1.3 fusion.31
  443.6 0.0 all-gather.3.cloned.1.call-start
  443.7 22.1 %reduce-scatter.5.cloned.1.call-done = f32[729,72]{0,1:T(8,128)} async-done(((f32[729,288]{0,1:T(8,128)}), f32[729,72]{0,1:T(8,128)}) %reduce-scatter.5.cloned.1.call-update) | async-done | bytes 209968 | tf_op jit(solution)/shard_map/reduce_scatter | solution.py:187
  465.8 1.0 fusion.29
  466.8 1.7 multiply_convert_fusion.1
  468.5 0.5 fusion.9
  469.0 0.3 convolution_multiply_fusion.1
  469.3 0.1 copy-done.12
  469.5 0.6 fusion.51
  470.1 0.8 pad_maximum_fusion
  470.9 0.2 all-reduce.18.cloned.1.call-start
  471.1 3.4 fusion.58
  474.5 1.9 fusion.45
  476.5 26.4 %all-gather.3.cloned.1.call-done = bf16[729,864]{0,1:T(8,128)(2,1)} async-done(((bf16[729,216]{0,1:T(8,128)(2,1)}), bf16[729,864]{0,1:T(8,128)(2,1)}) %all-gather.3.cloned.1.call-update) | async-done | bytes 1259728 | tf_op jit(solution)/shard_map/all_gather | solution.py:205
  502.9 2.9 fusion.61
  505.8 0.0 all-reduce.22.cloned.1.call-start
  505.9 3.4 fusion.62
  509.3 1.2 fusion.24
  510.5 1.6 fusion.41
  512.2 0.1 maximum_bitcast_fusion
  512.2 38.8 %all-reduce.18.cloned.1.call-done = (f32[729,288]{0,1:T(8,128)}, f32[729,288]{0,1:T(8,128)}) async-done(((f32[729,288]{0,1:T(8,128)}, f32[729,288]{0,1:T(8,128)}), (f32[729,288]{0,1:T(8,128)}, f32[729,288]{0,1:T(8,128)})) %all-reduce.18.cloned.1.call-update) | async-done | bytes 1679632 | tf_op jit(solution)/shard_map/psum | solution.py:45
  551.1 1.6 fusion.21
  552.7 9.0 %all-reduce.6 = (f32[288]{0:T(512)}, f32[288]{0:T(512)}, f32[1,1,144]{2,1,0:T(1,128)}, f32[288]{0:T(512)}, f32[288]{0:T(512)}, /*index=5*/f32[288]{0:T(512)}, f32[1076]{0:T(1024)}, f32[288]{0:T(512)}) all-reduce(f32[288]{0:T(512)S(1)} %get-tuple-element.64, ...), channel_id=1, replica_groups=mesh['dp'=2,'row'=4,'col'=4] {'dp'}, use_global_device_ids=true, to_apply=%region_26.27 | all-reduce | flops 2948 | bytes 23584 | tf_op jit(solution)/shard_map/psum | solution.py:224
  561.7 11.8 %all-reduce.1 = (f32[729,1]{0,1:T(1,128)S(1)}, f32[729,1]{0,1:T(1,128)S(1)}) all-reduce(f32[729,1]{0,1:T(1,128)S(1)} %broadcast_in_dim.65, f32[729,1]{0,1:T(1,128)S(1)} %broadcast_in_dim.64), channel_id=1, replica_groups=mesh['dp'=2,'row'=4,'col'=4] {'row'}, use_global_device_ids=true, to_apply=%region_24.25 | all-reduce | flops 1458 | bytes 11664 | tf_op jit(solution)/shard_map/psum | solution.py:41
  573.5 2.2 add_convert_fusion
  575.7 1.2 fusion.20
  576.9 84.5 %all-reduce.22.cloned.1.call-done = (f32[288,864]{1,0:T(8,128)}, f32[288,288]{1,0:T(8,128)}, f32[288,1076]{1,0:T(8,128)}, f32[1076,288]{0,1:T(8,128)}) async-done(((f32[288,864]{1,0:T(8,128)}, f32[288,288]{1,0:T(8,128)}, f32[288,1076]{1,0:T(8,128)}, f32[1076,288]{0,1:T(8,128)}), (f32[288,864]{1,0:T(8,128)}, f32[288,288]{1,0:T(8,128)}, f32[288,1076]{1,0:T(8,128)}, ...) | async-done | bytes 3806224 | tf_op jit(solution)/shard_map/psum | solution.py:224
  661.5 2.4 copy.46
  663.9 0.8 copy.47
  664.6 1.1 copy.48
  665.7 1.1 copy.49
  (77 shorter events, 0.4 us)
Async XLA Ops:
  7.2 138.9 %copy-start = (bf16[288,1076]{1,0:T(8,128)(2,1)S(1)}, bf16[288,1076]{1,0:T(8,128)(2,1)}, u32[]{:S(2)}) copy-start(bf16[288,1076]{1,0:T(8,128)(2,1)} %param.23) | copy-start | bytes 1859332
  7.2 69.9 %reduce-scatter.3.cloned.1.call-start = ((), (), s32[]{:S(2)}) async-start(), calls=%async_computation.2 | async-start | bytes 3317760 | tf_op jit(solution)/shard_map/reduce_scatter | solution.py:133
  22.2 3.9 copy-start.28
  26.0 105.9 %all-reduce.14.cloned.1.call-start = ((), (), s32[]{:S(2)}) async-start(), calls=%async_computation.3 | async-start | bytes 1769472 | tf_op jit(solution)/shard_map/psum | solution.py:45
  78.3 1.1 copy-start.9
  78.3 16.9 %copy-start.18 = (bf16[288,288]{1,0:T(8,128)(2,1)S(1)}, bf16[288,288]{1,0:T(8,128)(2,1)}, u32[]{:S(2)}) copy-start(bf16[288,288]{1,0:T(8,128)(2,1)} %param.19) | copy-start | bytes 497668
  94.4 0.8 copy-start.6
  96.6 35.3 %copy-start.4 = (bf16[729,288]{0,1:T(8,128)(2,1)S(1)}, bf16[729,288]{0,1:T(8,128)(2,1)}, u32[]{:S(2)}) copy-start(bf16[729,288]{0,1:T(8,128)(2,1)} %param.14) | copy-start | bytes 1259716
  96.6 35.3 %copy-start.24 = (f32[288]{0:T(512)S(1)}, f32[288]{0:T(512)}, u32[]{:S(2)}) copy-start(f32[288]{0:T(512)} %param.20) | copy-start | bytes 3460
  96.6 285.3 %all-reduce.20.cloned.1.call-start = ((), (), s32[]{:S(2)}) async-start(), calls=%async_computation.8 | async-start | bytes 13271040 | tf_op jit(solution)/shard_map/psum | solution.py:49
  100.7 45.4 %copy-start.22 = (f32[288]{0:T(512)S(1)}, f32[288]{0:T(512)}, u32[]{:S(2)}) copy-start(f32[288]{0:T(512)} %param.21) | copy-start | bytes 3460
  100.7 45.4 %copy-start.25 = (f32[288]{0:T(512)S(1)}, f32[288]{0:T(512)}, u32[]{:S(2)}) copy-start(f32[288]{0:T(512)} %param.22) | copy-start | bytes 3460
  150.2 231.7 %copy-start.23 = (f32[1076]{0:T(1024)S(1)}, f32[1076]{0:T(1024)}, u32[]{:S(2)}) copy-start(f32[1076]{0:T(1024)} %param.24) | copy-start | bytes 12916
  150.2 275.2 %all-reduce.16.cloned.1.call-start = ((), (), s32[]{:S(2)}) async-start(), calls=%async_computation.4 | async-start | bytes 1769472 | tf_op jit(solution)/shard_map/psum | solution.py:45
  387.8 1.2 copy-start.13
  390.7 75.1 %reduce-scatter.5.cloned.1.call-start = ((), (), s32[]{:S(2)}) async-start(), calls=%async_computation.5 | async-start | bytes 1105920 | tf_op jit(solution)/shard_map/reduce_scatter | solution.py:187
  439.1 3.2 copy-start.19
  441.3 1.0 copy-start.2
  443.6 59.2 %all-gather.3.cloned.1.call-start = ((), (), s32[]{:S(2)}) async-start(), calls=%async_computation.6 | async-start | bytes 1658880 | tf_op jit(solution)/shard_map/all_gather | solution.py:205
  465.8 2.7 copy-start.10
  468.5 0.9 copy-start.12
  470.9 80.2 %all-reduce.18.cloned.1.call-start = ((), (), s32[]{:S(2)}) async-start(), calls=%async_computation.7 | async-start | bytes 3538944 | tf_op jit(solution)/shard_map/psum | solution.py:45
  471.1 3.4 copy-start.1
  471.1 3.4 copy-start.14
  474.5 28.3 %copy-start.11 = (bf16[288,864]{1,0:T(8,128)(2,1)S(1)}, bf16[288,864]{1,0:T(8,128)(2,1)}, u32[]{:S(2)}) copy-start(bf16[288,864]{1,0:T(8,128)(2,1)} %param.17) | copy-start | bytes 1492996
  476.4 29.4 %copy-start.5 = (bf16[729,288]{0,1:T(8,128)(2,1)S(1)}, bf16[729,288]{0,1:T(8,128)(2,1)}, u32[]{:S(2)}) copy-start(bf16[729,288]{0,1:T(8,128)(2,1)} %param.27) | copy-start | bytes 1259716
  505.8 3.6 copy-start.3
  505.8 4.7 copy-start.21
  505.8 4.7 copy-start.26
  505.8 155.7 %all-reduce.22.cloned.1.call-start = ((), (), s32[]{:S(2)}) async-start(), calls=%async_computation.9 | async-start | bytes 8257536 | tf_op jit(solution)/shard_map/psum | solution.py:224
  505.8 3.5 copy-start.7
  505.9 4.6 copy-start.17
  512.1 61.4 %copy-start.27 = (f32[288]{0:T(512)S(1)}, f32[288]{0:T(512)}, u32[]{:S(2)}) copy-start(f32[288]{0:T(512)} %param.26) | copy-start | bytes 3460
  573.5 2.3 copy-start.8
  661.5 2.4 copy-start.20
  661.5 3.1 copy-start.16
  663.9 1.8 copy-start.15
Sparse Core Ops, SparseCore 0:
  26.1 50.9 reduce-scatter.2
  96.7 35.1 all-reduce.13
  150.4 231.4 all-reduce.19
  390.8 34.5 all-reduce.15
  443.7 22.0 reduce-scatter.4
  471.0 31.8 all-gather.2
  505.9 45.1 all-reduce.17
  554.9 106.5 all-reduce.21
where the time goes:
time: 674 us
  waiting for transfers between devices  520 us (77%)
  blocking collectives  73.1 us (11%)
  matrix products  34.8 us (5%)
  other arithmetic  21.7 us (3%)
  between operations  14.5 us (2%)
  local copies, waits for them, and re-layouts  8.61 us (1%)
    psum x1, waiting for transfers between devices, ff_total(): return lax.psum(partial_sum, 'row')  232 us
    psum x3, waiting for transfers between devices, col_total(): return lax.psum(partial_sum, 'col')  105 us
    psum x1, waiting for transfers between devices, body(): lax.psum((reduce_weight_grad, reduce_bias_grad, expand_weight_grad, expan...  84.5 us
    reduce_scatter x1, waiting for transfers between devices, body(): lax.psum_scatter(joint_part, 'row', scatter_dimension=1, tiled=True)  50.8 us
    psum x4, blocking collectives, row_totals(): return lax.psum((first, second), 'row')  49.2 us
    all_gather x1, waiting for transfers between devices, body(): joint_group = lax.all_gather(joint_grad, 'row', axis=1, tiled=True)  26.4 us
    reduce_scatter x1, waiting for transfers between devices, body(): lax.psum_scatter(contract_cols(mixed_low, merge_weight), 'row', scatter_d...  22.1 us
    all_gather x1, blocking collectives, body(): context_group = lax.all_gather(context_flat, 'row', axis=1, tiled=True)  15 us
  transfers between devices with their start and end apart: 8, of which 8 were waited for; matrix products, arithmetic and copies ran while one was open for 3% of the time, Pallas kernels for 0%

commit v1 on v0

--- a/solution.py
+++ b/solution.py
@@ -46,7 +46,7 @@
 
 
 def ff_total(partial_sum):
-    return lax.psum(partial_sum, "row")
+    return jnp.sum(lax.all_gather(partial_sum, "row"), axis=0)
 
 
 def norm_forward(values, norm_gain, norm_shift):

time: 674 us -> 891 us (1.32)
  waiting for transfers between devices: 520 us -> 722 us
  other arithmetic: 21.7 us -> 37.1 us
    all_gather x0 -> x2, waiting for transfers between devices: none -> 434 us  [ff_total(): return jnp.sum(lax.all_gather(partial_sum, 'row'), axis=0)]
    psum x1 -> x0, waiting for transfers between devices: 232 us -> none  [ff_total(): return lax.psum(partial_sum, 'row')]
    reduce_sum x0 -> x2, other arithmetic: none -> 15.6 us  [ff_total(): return jnp.sum(lax.all_gather(partial_sum, 'row'), axis=0)]
  transfers between devices with their start and end apart: 8 -> 9, of which waited for: 8 -> 9; matrix products, arithmetic and copies ran while one was open for 3% -> 4% of each run, Pallas kernels for 0% -> 0%
where the time goes in v1:
time: 891 us
  waiting for transfers between devices  722 us (81%)
  blocking collectives  73.3 us (8%)
  other arithmetic  37.1 us (4%)
  matrix products  34.6 us (4%)
  between operations  14.3 us (2%)
    all_gather x2, waiting for transfers between devices, ff_total(): return jnp.sum(lax.all_gather(partial_sum, 'row'), axis=0)  434 us
    psum x3, waiting for transfers between devices, col_total(): return lax.psum(partial_sum, 'col')  104 us
    psum x1, waiting for transfers between devices, body(): lax.psum((reduce_weight_grad, reduce_bias_grad, expand_weight_grad, expan...  84.5 us
    reduce_scatter x1, waiting for transfers between devices, body(): lax.psum_scatter(joint_part, 'row', scatter_dimension=1, tiled=True)  50.8 us
    psum x4, blocking collectives, row_totals(): return lax.psum((first, second), 'row')  49.3 us
    all_gather x1, waiting for transfers between devices, body(): joint_group = lax.all_gather(joint_grad, 'row', axis=1, tiled=True)  26.6 us
    reduce_scatter x1, waiting for transfers between devices, body(): lax.psum_scatter(contract_cols(mixed_low, merge_weight), 'row', scatter_d...  22.1 us
  transfers between devices with their start and end apart: 9, of which 9 were waited for; matrix products, arithmetic and copies ran while one was open for 4% of the time, Pallas kernels for 0%

profile of v1, /device:TPU:0, one launch (start us, length us, event | category | flops | bytes accessed | tf_op | source)
XLA Modules:
  0.0 890.5 jit_solution(6981462693697986368)
XLA Ops:
  7.2 1.2 convert_reduce_fusion.1
  8.5 13.7 %all-reduce.4 = (f32[729,1]{0,1:T(1,128)S(1)}, f32[729,1]{0,1:T(1,128)S(1)}) all-reduce(f32[729,1]{0,1:T(1,128)S(1)} %broadcast_in_dim.57, f32[729,1]{0,1:T(1,128)S(1)} %broadcast_in_dim.58), channel_id=1, replica_groups=mesh['dp'=2,'row'=4,'col'=4] {'row'}, use_global_device_ids=true, to_apply=%region_1.0 | all-reduce | flops 1458 | bytes 11664 | tf_op jit(solution)/shard_map/psum | solution.py:41
  22.2 3.7 fusion.43
  26.0 0.0 all-reduce.12.cloned.1.call-start
  26.0 0.1 pad.6.clone
  26.1 0.1 fusion.52
  26.2 0.1 pad_maximum_fusion.1
  26.3 50.8 %reduce-scatter.3.cloned.1.call-done = f32[729,216]{0,1:T(8,128)} async-done(((f32[729,864]{0,1:T(8,128)}), f32[729,216]{0,1:T(8,128)}) %reduce-scatter.3.cloned.1.call-update) | async-done | bytes 629872 | tf_op jit(solution)/shard_map/reduce_scatter | solution.py:133
  77.1 1.2 fusion.28
  78.3 0.6 exponential_reduce_fusion
  78.9 0.5 convolution_convert_fusion
  79.5 15.0 %all-gather = bf16[729,1,288]{0,2,1:T(8,128)(2,1)S(1)} all-gather(bf16[729,1,72]{0,2,1:T(8,128)(2,1)S(1)} %bitcast.76), channel_id=2, replica_groups=mesh['dp'=2,'row'=4,'col'=4] {'row'}, dimensions={2}, use_global_device_ids=true | all-gather | bytes 524880 | tf_op jit(solution)/shard_map/all_gather | solution.py:153
  94.5 0.8 copy-done.6
  95.2 1.3 fusion.26
  96.6 0.0 all-gather.13.cloned.1.call-start
  96.7 3.9 convolution_bitcast_fusion
  100.6 31.4 %all-reduce.12.cloned.1.call-done = f32[729,288]{0,1:T(8,128)} async-done(((f32[729,288]{0,1:T(8,128)}), f32[729,288]{0,1:T(8,128)}) %all-reduce.12.cloned.1.call-update) | async-done | bytes 839824 | tf_op jit(solution)/shard_map/psum | solution.py:45
  132.0 2.3 fusion.46
  134.4 11.8 %all-reduce.3 = (f32[729,1]{0,1:T(1,128)S(1)}, f32[729,1]{0,1:T(1,128)S(1)}) all-reduce(f32[729,1]{0,1:T(1,128)S(1)} %broadcast_in_dim.60, f32[729,1]{0,1:T(1,128)S(1)} %broadcast_in_dim.61), channel_id=1, replica_groups=mesh['dp'=2,'row'=4,'col'=4] {'row'}, use_global_device_ids=true, to_apply=%region_8.9 | all-reduce | flops 1458 | bytes 11664 | tf_op jit(solution)/shard_map/psum | solution.py:41
  146.2 4.1 convolution_bitcast_fusion.1
  150.3 0.0 all-reduce.14.cloned.1.call-start
  150.4 212.8 %all-gather.13.cloned.1.call-done = f32[4,729,1076]{1,2,0:T(8,128)} async-done(((f32[1,729,1076]{1,2,0:T(8,128)}), f32[4,729,1076]{1,2,0:T(8,128)}) %all-gather.13.cloned.1.call-update) | async-done | bytes 12550480 | tf_op jit(solution)/shard_map/all_gather | solution.py:49
  363.2 7.8 reduce_sum.191
  371.0 221.2 %all-gather.11.cloned.1.call-done = f32[4,729,1076]{1,2,0:T(8,128)} async-done(((f32[1,729,1076]{1,2,0:T(8,128)}), f32[4,729,1076]{1,2,0:T(8,128)}) %all-gather.11.cloned.1.call-update) | async-done | bytes 12550480 | tf_op jit(solution)/shard_map/all_gather | solution.py:49
  592.2 7.8 reduce_sum.190
  600.0 5.9 convert_reduce_fusion
  606.0 1.2 copy-done.15
  607.2 1.7 fusion.58
  608.9 0.0 reduce-scatter.5.cloned.1.call-start
  608.9 33.8 %all-reduce.14.cloned.1.call-done = f32[729,288]{0,1:T(8,128)} async-done(((f32[729,288]{0,1:T(8,128)}), f32[729,288]{0,1:T(8,128)}) %all-reduce.14.cloned.1.call-update) | async-done | bytes 839824 | tf_op jit(solution)/shard_map/psum | solution.py:45
  642.8 1.8 multiply_reduce_fusion
  644.6 12.0 %all-reduce.2 = (f32[729,1]{0,1:T(1,128)S(1)}, f32[729,1]{0,1:T(1,128)S(1)}) all-reduce(f32[729,1]{0,1:T(1,128)S(1)} %broadcast_in_dim.63, f32[729,1]{0,1:T(1,128)S(1)} %broadcast_in_dim.62), channel_id=1, replica_groups=mesh['dp'=2,'row'=4,'col'=4] {'row'}, use_global_device_ids=true, to_apply=%region_18.19 | all-reduce | flops 1458 | bytes 11664 | tf_op jit(solution)/shard_map/psum | solution.py:41
  656.7 2.0 fusion.48
  658.7 0.9 copy-done.3
  659.6 1.3 fusion.31
  661.0 22.1 %reduce-scatter.5.cloned.1.call-done = f32[729,72]{0,1:T(8,128)} async-done(((f32[729,288]{0,1:T(8,128)}), f32[729,72]{0,1:T(8,128)}) %reduce-scatter.5.cloned.1.call-update) | async-done | bytes 209968 | tf_op jit(solution)/shard_map/reduce_scatter | solution.py:187
  683.1 1.0 fusion.29
  684.1 1.6 multiply_convert_fusion.1
  685.7 0.5 fusion.9
  686.2 0.3 convolution_multiply_fusion.1
  686.5 0.1 copy-done.12
  686.7 0.6 fusion.50
  687.3 0.8 pad_maximum_fusion
  688.1 0.0 all-reduce.16.cloned.1.call-start
  688.2 3.4 fusion.57
  691.6 1.9 fusion.45
  693.5 26.6 %all-gather.9.cloned.1.call-done = bf16[729,864]{0,1:T(8,128)(2,1)} async-done(((bf16[729,216]{0,1:T(8,128)(2,1)}), bf16[729,864]{0,1:T(8,128)(2,1)}) %all-gather.9.cloned.1.call-update) | async-done | bytes 1259728 | tf_op jit(solution)/shard_map/all_gather | solution.py:205
  720.1 2.9 fusion.59
  723.0 0.0 all-reduce.18.cloned.1.call-start
  723.1 3.5 fusion.60
  726.6 1.2 fusion.24
  727.7 1.6 fusion.41
  729.4 0.1 maximum_bitcast_fusion
  729.5 38.8 %all-reduce.16.cloned.1.call-done = (f32[729,288]{0,1:T(8,128)}, f32[729,288]{0,1:T(8,128)}) async-done(((f32[729,288]{0,1:T(8,128)}, f32[729,288]{0,1:T(8,128)}), (f32[729,288]{0,1:T(8,128)}, f32[729,288]{0,1:T(8,128)})) %all-reduce.16.cloned.1.call-update) | async-done | bytes 1679632 | tf_op jit(solution)/shard_map/psum | solution.py:45
  768.3 1.6 fusion.21
  769.9 9.0 %all-reduce.5 = (f32[288]{0:T(512)}, f32[288]{0:T(512)}, f32[1,1,144]{2,1,0:T(1,128)}, f32[288]{0:T(512)}, f32[288]{0:T(512)}, /*index=5*/f32[288]{0:T(512)}, f32[1076]{0:T(1024)}, f32[288]{0:T(512)}) all-reduce(f32[288]{0:T(512)S(1)} %get-tuple-element.64, ...), channel_id=1, replica_groups=mesh['dp'=2,'row'=4,'col'=4] {'dp'}, use_global_device_ids=true, to_apply=%region_26.27 | all-reduce | flops 2948 | bytes 23584 | tf_op jit(solution)/shard_map/psum | solution.py:224
  778.9 11.8 %all-reduce.1 = (f32[729,1]{0,1:T(1,128)S(1)}, f32[729,1]{0,1:T(1,128)S(1)}) all-reduce(f32[729,1]{0,1:T(1,128)S(1)} %broadcast_in_dim.65, f32[729,1]{0,1:T(1,128)S(1)} %broadcast_in_dim.64), channel_id=1, replica_groups=mesh['dp'=2,'row'=4,'col'=4] {'row'}, use_global_device_ids=true, to_apply=%region_24.25 | all-reduce | flops 1458 | bytes 11664 | tf_op jit(solution)/shard_map/psum | solution.py:41
  790.7 2.2 add_convert_fusion
  792.9 1.2 fusion.20
  794.1 84.5 %all-reduce.18.cloned.1.call-done = (f32[288,864]{1,0:T(8,128)}, f32[288,288]{1,0:T(8,128)}, f32[288,1076]{1,0:T(8,128)}, f32[1076,288]{0,1:T(8,128)}) async-done(((f32[288,864]{1,0:T(8,128)}, f32[288,288]{1,0:T(8,128)}, f32[288,1076]{1,0:T(8,128)}, f32[1076,288]{0,1:T(8,128)}), (f32[288,864]{1,0:T(8,128)}, f32[288,288]{1,0:T(8,128)}, f32[288,1076]{1,0:T(8,128)}, ...) | async-done | bytes 3806224 | tf_op jit(solution)/shard_map/psum | solution.py:224
  878.7 2.4 copy.45
  881.1 0.8 copy.46
  881.8 1.1 copy.47
  882.9 1.1 copy.48
  (86 shorter events, 0.6 us)
Async XLA Ops:
  7.2 139.0 %copy-start = (bf16[288,1076]{1,0:T(8,128)(2,1)S(1)}, bf16[288,1076]{1,0:T(8,128)(2,1)}, u32[]{:S(2)}) copy-start(bf16[288,1076]{1,0:T(8,128)(2,1)} %param.23) | copy-start | bytes 1859332
  7.2 69.9 %reduce-scatter.3.cloned.1.call-start = ((), (), s32[]{:S(2)}) async-start(), calls=%async_computation.2 | async-start | bytes 3317760 | tf_op jit(solution)/shard_map/reduce_scatter | solution.py:133
  22.2 3.9 copy-start.30
  26.0 106.1 %all-reduce.12.cloned.1.call-start = ((), (), s32[]{:S(2)}) async-start(), calls=%async_computation.3 | async-start | bytes 1769472 | tf_op jit(solution)/shard_map/psum | solution.py:45
  78.3 1.1 copy-start.9
  78.3 16.9 %copy-start.20 = (bf16[288,288]{1,0:T(8,128)(2,1)S(1)}, bf16[288,288]{1,0:T(8,128)(2,1)}, u32[]{:S(2)}) copy-start(bf16[288,288]{1,0:T(8,128)(2,1)} %param.19) | copy-start | bytes 497668
  78.9 17.7 %copy-start.13 = (bf16[729,288]{0,1:T(8,128)(2,1)S(1)}, bf16[729,288]{0,1:T(8,128)(2,1)}, u32[]{:S(2)}) copy-start(bf16[729,288]{0,1:T(8,128)(2,1)} %param.27) | copy-start | bytes 1259716
  94.5 0.8 copy-start.6
  96.6 266.6 %all-gather.13.cloned.1.call-start = ((), (), s32[]{:S(2)}) async-start(), calls=%async_computation.8 | async-start | bytes 16588800 | tf_op jit(solution)/shard_map/all_gather | solution.py:49
  100.5 31.5 %copy-start.5 = (bf16[729,288]{0,1:T(8,128)(2,1)S(1)}, bf16[729,288]{0,1:T(8,128)(2,1)}, u32[]{:S(2)}) copy-start(bf16[729,288]{0,1:T(8,128)(2,1)} %param.14) | copy-start | bytes 1259716
  100.6 31.5 %copy-start.26 = (f32[288]{0:T(512)S(1)}, f32[288]{0:T(512)}, u32[]{:S(2)}) copy-start(f32[288]{0:T(512)} %param.20) | copy-start | bytes 3460
  100.6 45.7 %copy-start.24 = (f32[288]{0:T(512)S(1)}, f32[288]{0:T(512)}, u32[]{:S(2)}) copy-start(f32[288]{0:T(512)} %param.21) | copy-start | bytes 3460
  100.6 45.7 %copy-start.27 = (f32[288]{0:T(512)S(1)}, f32[288]{0:T(512)}, u32[]{:S(2)}) copy-start(f32[288]{0:T(512)} %param.22) | copy-start | bytes 3460
  100.6 491.7 %all-gather.11.cloned.1.call-start = ((), (), s32[]{:S(2)}) async-start(), calls=%async_computation.7 | async-start | bytes 16588800 | tf_op jit(solution)/shard_map/all_gather | solution.py:49
  150.3 492.4 %all-reduce.14.cloned.1.call-start = ((), (), s32[]{:S(2)}) async-start(), calls=%async_computation.4 | async-start | bytes 1769472 | tf_op jit(solution)/shard_map/psum | solution.py:45
  371.0 229.0 %copy-start.25 = (f32[1076]{0:T(1024)S(1)}, f32[1076]{0:T(1024)}, u32[]{:S(2)}) copy-start(f32[1076]{0:T(1024)} %param.24) | copy-start | bytes 12916
  606.0 1.2 copy-start.15
  608.8 47.8 %copy-start.14 = (bf16[729,288]{0,1:T(8,128)(2,1)S(1)}, bf16[729,288]{0,1:T(8,128)(2,1)}, u32[]{:S(2)}) copy-start(bf16[729,288]{0,1:T(8,128)(2,1)} %param.27) | copy-start | bytes 1259716
  608.9 50.8 %copy-start.21 = (bf16[288,288]{1,0:T(8,128)(2,1)S(1)}, bf16[288,288]{1,0:T(8,128)(2,1)}, u32[]{:S(2)}) copy-start(bf16[288,288]{1,0:T(8,128)(2,1)} %param.19) | copy-start | bytes 497668
  608.9 74.3 %reduce-scatter.5.cloned.1.call-start = ((), (), s32[]{:S(2)}) async-start(), calls=%async_computation.5 | async-start | bytes 1105920 | tf_op jit(solution)/shard_map/reduce_scatter | solution.py:187
  658.7 0.9 copy-start.3
  658.7 25.4 %copy-start.10 = (bf16[1,729,1,216]{1,3,2,0:T(8,128)(2,1)S(1)}, bf16[1,729,1,216]{1,3,2,0:T(8,128)(2,1)}, u32[]{:S(2)}) copy-start(bf16[1,729,1,216]{1,3,2,0:T(8,128)(2,1)} %copy-done.9) | copy-start | bytes 944788
  660.9 59.1 %all-gather.9.cloned.1.call-start = ((), (), s32[]{:S(2)}) async-start(), calls=%async_computation.6 | async-start | bytes 1658880 | tf_op jit(solution)/shard_map/all_gather | solution.py:205
  685.7 0.9 copy-start.12
  688.1 80.2 %all-reduce.16.cloned.1.call-start = ((), (), s32[]{:S(2)}) async-start(), calls=%async_computation.9 | async-start | bytes 3538944 | tf_op jit(solution)/shard_map/psum | solution.py:45
  688.1 3.4 copy-start.2
  688.1 3.4 copy-start.16
  691.6 28.5 %copy-start.11 = (bf16[288,864]{1,0:T(8,128)(2,1)S(1)}, bf16[288,864]{1,0:T(8,128)(2,1)}, u32[]{:S(2)}) copy-start(bf16[288,864]{1,0:T(8,128)(2,1)} %param.17) | copy-start | bytes 1492996
  723.0 3.6 copy-start.4
  723.0 3.6 copy-start.7
  723.0 4.8 copy-start.23
  723.0 4.7 copy-start.28
  723.0 155.7 %all-reduce.18.cloned.1.call-start = ((), (), s32[]{:S(2)}) async-start(), calls=%async_computation.10 | async-start | bytes 8257536 | tf_op jit(solution)/shard_map/psum | solution.py:224
  723.0 4.7 copy-start.19
  729.4 61.3 %copy-start.29 = (f32[288]{0:T(512)S(1)}, f32[288]{0:T(512)}, u32[]{:S(2)}) copy-start(f32[288]{0:T(512)} %param.26) | copy-start | bytes 3460
  790.7 2.3 copy-start.8
  878.7 2.4 copy-start.22
  878.7 3.1 copy-start.18
  881.1 1.8 copy-start.17
  881.1 2.9 copy-start.1
Sparse Core Ops, SparseCore 0:
  26.1 50.9 reduce-scatter.2
  96.7 35.2 all-reduce.11
  133.6 229.5 all-gather.12
  364.6 227.6 all-gather.10
  609.0 33.7 all-reduce.13
  661.1 22.0 reduce-scatter.4
  688.2 31.8 all-gather.8
  723.1 45.1 all-reduce.15
  772.1 106.5 all-reduce.17
